TPU v7x, 32 devices: a whole 2x2x4 slice. The times are simulated.
32 devices in a mesh: batch: 4 (over y, x), corpus: 8 (over z, core).
Axes of the slice: x: 2, y: 2, z: 4, core: 2. Of those that a mesh axis runs over, the one named last changes fastest.
Arguments:
- states: bfloat16 [4096, 4096], P('batch', 'corpus'), may hold values from -6 to 6
- norm_gain: float32 [4096], replicated, may hold values from 0.25 to 1.75
- gate_weight: bfloat16 [4096, 12288], P('batch', 'corpus'), may hold values from -0.09375 to 0.09375
- up_weight: bfloat16 [4096, 12288], P('batch', 'corpus'), may hold values from -0.09375 to 0.09375
- down_weight: bfloat16 [12288, 4096], P('corpus', 'batch'), may hold values from -0.0546875 to 0.0546875
- final_gain: float32 [4096], replicated, may hold values from 0.25 to 1.75
- hash_weight: bfloat16 [4096, 1024], replicated, may hold values from -0.75 to 0.75
- query_bits: bfloat16 [4096, 1024], replicated, may hold values from -1 to 1
- slot_map: int32 [64], replicated, may hold values from 0 to 63, each once
- query_index: int32 [4096, 100], replicated, may hold values from 0 to 63
Outputs:
- scores: float32 [4096, 100], P(('batch', 'corpus'))
Inputs may be any that keep to these rules, and one draw needn't show every extreme that they name: `slot_map`: each corpus entry is named by exactly one document.
All inputs are finite; a program needn't handle non-finite values.
Results may differ from a plain program's by a relative error of at most 0.017.
Values may be sent and summed in bfloat16 or wider, within the bound.
A program may use at most 192 MiB of HBM per device.

v0:
```python
import jax
import jax.numpy as jnp
from jax import lax
from jax.sharding import PartitionSpec as P

DOC_LEN = 64
CODE = 1024
NQ = 4096


def rms(values, gain):
    return values * lax.rsqrt(jnp.mean(values * values, axis=-1, keepdims=True) + 1e-06) * gain


def add_rows(left, piece):
    return jnp.dot(left, piece, preferred_element_type=jnp.float32)


def local(
    states,
    norm_gain,
    gate_weight,
    up_weight,
    down_weight,
    final_gain,
    hash_weight,
    query_bits,
    slot_map,
    query_index,
):
    corpus_count = lax.axis_size("corpus")
    devices = lax.axis_size("batch") * corpus_count
    flat_index = lax.axis_index("batch") * corpus_count + lax.axis_index("corpus")
    whole = lax.all_gather(states, "corpus", axis=1, tiled=True)
    normed = rms(whole.astype(jnp.float32), norm_gain).astype(jnp.bfloat16)

    def add_one(piece):
        return add_rows(normed, piece)

    gate = add_one(lax.all_gather(gate_weight, "batch", axis=0, tiled=True))
    up = add_one(lax.all_gather(up_weight, "batch", axis=0, tiled=True))
    hidden = (jax.nn.silu(gate) * up).astype(jnp.bfloat16)
    terms = jnp.dot(
        hidden,
        lax.all_gather(down_weight, "batch", axis=1, tiled=True),
        preferred_element_type=jnp.float32,
    )
    ffn = lax.psum_scatter(
        terms.astype(jnp.bfloat16), "corpus", scatter_dimension=0, tiled=True
    ).astype(jnp.float32)
    own_rows = ffn.shape[0]
    mine = lax.dynamic_slice_in_dim(whole, lax.axis_index("corpus") * own_rows, own_rows, 0)
    resid = mine.astype(jnp.float32) + ffn
    finals = rms(resid, final_gain)
    owned_docs = own_rows // DOC_LEN
    pooled = jnp.mean(finals.reshape(owned_docs, DOC_LEN, finals.shape[1]), axis=1).astype(
        jnp.bfloat16
    )
    codes = jnp.tanh(jnp.dot(pooled, hash_weight, preferred_element_type=jnp.float32)).astype(
        jnp.bfloat16
    )
    doc_total = owned_docs * devices
    scale = 1.0 / jnp.sqrt(jnp.float32(CODE))
    gathered = lax.all_gather(codes, ("batch", "corpus"), axis=0, tiled=True)
    placing = (slot_map[:, None] == jnp.arange(doc_total, dtype=jnp.int32)[None, :]).astype(
        jnp.bfloat16
    )
    corpus = jnp.einsum("ds,dc->sc", placing, gathered, preferred_element_type=jnp.float32).astype(
        jnp.bfloat16
    )
    query_rows = NQ // devices
    my_bits = lax.dynamic_slice_in_dim(query_bits, flat_index * query_rows, query_rows, 0)
    my_index = lax.dynamic_slice_in_dim(query_index, flat_index * query_rows, query_rows, 0)
    table = jnp.dot(my_bits, corpus.T, preferred_element_type=jnp.float32) * scale
    scores = jnp.take_along_axis(table, my_index, axis=1)
    return scores


def solution(mesh):
    placed = (
        P("batch", "corpus"),
        P(),
        P("batch", "corpus"),
        P("batch", "corpus"),
        P("corpus", "batch"),
        P(),
        P(),
        P(),
        P(),
        P(),
    )
    return jax.shard_map(
        local, mesh=mesh, in_specs=placed, out_specs=P(("batch", "corpus"), None), check_vma=False
    )
```

profile of v0, /device:TPU:0, one launch (start us, length us, event | category | flops | bytes accessed | tf_op | source)
XLA Modules:
  0.0 712.4 jit_solution(285428027022941697)
XLA Ops:
  6.5 0.0 copy-start
  6.5 0.0 all-gather.6.cloned.1.call-start
  6.5 0.7 all-gather.6.cloned.1.call-update
  7.3 0.0 copy-start.3
  7.3 0.0 all-gather.8.cloned.1.call-start
  7.3 0.7 all-gather.8.cloned.1.call-update
  8.0 0.0 all-gather.10.cloned.1.call-start
  8.1 0.7 all-gather.10.cloned.1.call-update
  8.8 0.0 all-gather.12.cloned.1.call-start
  8.8 0.5 all-gather.12.cloned.1.call-update
  9.3 0.0 reduce-scatter.2.cloned.1.call-start
  9.4 84.4 %all-gather.6.cloned.1.call-done = bf16[1024,4096]{1,0:T(8,128)(2,1)} async-done(((bf16[1024,512]{1,0:T(8,128)(2,1)}), bf16[1024,4096]{1,0:T(8,128)(2,1)}) %all-gather.6.cloned.1.call-update) | async-done | bytes 8388624 | tf_op jit(solution)/shard_map/all_gather | solution.py:34
  93.7 5.1 fusion
  98.8 117.7 %all-gather.8.cloned.1.call-done = bf16[4096,1536]{1,0:T(8,128)(2,1)} async-done(((bf16[1024,1536]{1,0:T(8,128)(2,1)}), bf16[4096,1536]{1,0:T(8,128)(2,1)}) %all-gather.8.cloned.1.call-update) | async-done | bytes 12582928 | tf_op jit(solution)/shard_map/all_gather | solution.py:40
  216.5 0.0 copy-done.3
  216.5 19.7 %fusion.4 = f32[1024,1536]{1,0:T(8,128)} fusion(bf16[4096,1536]{1,0:T(8,128)(2,1)} %all-gather.8.cloned.1.call-done, bf16[1024,4096]{1,0:T(8,128)(2,1)} %all-gather.6.cloned.1.call-done, f32[4096]{0:T(1024)S(1)} %copy-done.3, f32[1024]{0:T(1024)S(1)} %add_rsqrt_fusion), kind=kOutput, calls=%fused_computation.8 | convolution fusion | flops 12901679104 | bytes 27283456 | tf_op jit(solution)/shard_map/dot_general | solution.py:16
  236.2 104.6 %all-gather.10.cloned.1.call-done = bf16[4096,1536]{1,0:T(8,128)(2,1)} async-done(((bf16[1024,1536]{1,0:T(8,128)(2,1)}), bf16[4096,1536]{1,0:T(8,128)(2,1)}) %all-gather.10.cloned.1.call-update) | async-done | bytes 12582928 | tf_op jit(solution)/shard_map/all_gather | solution.py:41
  340.7 20.6 %multiply_convert_fusion = bf16[1024,1536]{1,0:T(8,128)(2,1)} fusion(f32[1024,1536]{1,0:T(8,128)} %fusion.4, bf16[4096,1536]{1,0:T(8,128)(2,1)} %all-gather.10.cloned.1.call-done, bf16[1024,4096]{1,0:T(8,128)(2,1)} %all-gather.6.cloned.1.call-done, f32[4096]{0:T(1024)S(1)} %copy-done.3, f32[1024]{0:T(1024)S(1)} %add_rsqrt_fusion), kind=kOutput, calls=%fused_computation.7 | convolution fusion | flops 12911116288 | bytes 30429184 | tf_op jit(solution)/shard_map/dot_general | solution.py:16
  361.4 103.5 %all-gather.12.cloned.1.call-done = bf16[1536,4096]{1,0:T(8,128)(2,1)} async-done(((bf16[1536,1024]{1,0:T(8,128)(2,1)}), bf16[1536,4096]{1,0:T(8,128)(2,1)}) %all-gather.12.cloned.1.call-update) | async-done | bytes 12582928 | tf_op jit(solution)/shard_map/all_gather | solution.py:45
  464.9 19.1 %convolution_convert_fusion = bf16[1024,4096]{1,0:T(8,128)(2,1)} fusion(bf16[1024,1536]{1,0:T(8,128)(2,1)} %multiply_convert_fusion, bf16[1536,4096]{1,0:T(8,128)(2,1)} %all-gather.12.cloned.1.call-done), kind=kOutput, calls=%fused_computation.6 | convolution fusion | flops 12889096192 | bytes 24117248 | tf_op jit(solution)/shard_map/dot_general | solution.py:43
  483.9 0.0 copy-start.1
  483.9 0.0 reduce-scatter.2.cloned.1.call-update
  483.9 0.0 copy-done
  484.0 0.1 copy.15
  484.1 0.1 reshape.33
  484.2 89.4 %reduce-scatter.2.cloned.1.call-done = bf16[128,4096]{1,0:T(8,128)(2,1)} async-done(((bf16[1024,4096]{1,0:T(8,128)(2,1)}), bf16[128,4096]{1,0:T(8,128)(2,1)}) %reduce-scatter.2.cloned.1.call-update) | async-done | bytes 1048592 | tf_op jit(solution)/shard_map/reduce_scatter | solution.py:48
  573.6 2.0 multiply_reduce_fusion
  575.6 0.0 copy-done.1
  575.6 2.0 bitcast_reduce_fusion
  577.6 0.0 copy-start.2
  577.7 4.6 fusion.9
  582.2 39.5 %all-gather = bf16[32,2,1024]{2,1,0:T(2,128)(2,1)S(1)} all-gather(bf16[1,2,1024]{2,1,0:T(2,128)(2,1)S(1)} %fusion.9), channel_id=1, replica_groups=mesh['batch'=4,'corpus'=8] {'batch','corpus'}, dimensions={0}, use_global_device_ids=true | all-gather | bytes 135168 | tf_op jit(solution)/shard_map/all_gather | solution.py:64
  621.7 0.1 reshape.45
  621.8 0.0 copy-done.2
  621.8 1.4 fusion.7
  623.2 81.8 %gather_fusion = f32[12800]{0:T(1024)S(1)} fusion(f32[128,64]{0,1:T(8,128)S(1)} %fusion.7, s32[12800]{0:T(1024)S(1)} %reshape.33), kind=kCustom, calls=%fused_computation | custom fusion | bytes 204800 | tf_op jit(solution)/shard_map/jit(take_along_axis)/gather | solution.py:75
  705.0 0.1 reshape.36
  705.2 0.7 copy.14
  (5 shorter events, 0.1 us)
Async XLA Ops:
  6.5 477.4 %copy-start = (s32[4096,100]{0,1:T(8,128)S(1)}, s32[4096,100]{0,1:T(8,128)}, u32[]{:S(2)}) copy-start(s32[4096,100]{0,1:T(8,128)} %param.19) | copy-start | bytes 4915204
  6.5 87.2 %all-gather.6.cloned.1.call-start = ((), (), s32[]{:S(2)}) async-start(), calls=%async_computation.1 | async-start | bytes 9437184 | tf_op jit(solution)/shard_map/all_gather | solution.py:34
  7.3 209.2 %copy-start.3 = (f32[4096]{0:T(1024)S(1)}, f32[4096]{0:T(1024)}, u32[]{:S(2)}) copy-start(f32[4096]{0:T(1024)} %param.11) | copy-start | bytes 49156
  7.3 209.2 %all-gather.8.cloned.1.call-start = ((), (), s32[]{:S(2)}) async-start(), calls=%async_computation.2 | async-start | bytes 15728640 | tf_op jit(solution)/shard_map/all_gather | solution.py:40
  8.0 332.7 %all-gather.10.cloned.1.call-start = ((), (), s32[]{:S(2)}) async-start(), calls=%async_computation.3 | async-start | bytes 15728640 | tf_op jit(solution)/shard_map/all_gather | solution.py:41
  8.8 456.1 %all-gather.12.cloned.1.call-start = ((), (), s32[]{:S(2)}) async-start(), calls=%async_computation.4 | async-start | bytes 15728640 | tf_op jit(solution)/shard_map/all_gather | solution.py:45
  9.3 564.3 %reduce-scatter.2.cloned.1.call-start = ((), (), s32[]{:S(2)}) async-start(), calls=%async_computation.5 | async-start | bytes 9437184 | tf_op jit(solution)/shard_map/reduce_scatter | solution.py:48
  483.9 91.7 %copy-start.1 = (f32[4096]{0:T(1024)S(1)}, f32[4096]{0:T(1024)}, u32[]{:S(2)}) copy-start(f32[4096]{0:T(1024)} %param.15) | copy-start | bytes 49156
  577.6 44.1 %copy-start.2 = (s32[64]{0:T(128)S(1)}, s32[64]{0:T(128)}, u32[]{:S(2)}) copy-start(s32[64]{0:T(128)} %param.18) | copy-start | bytes 772
Sparse Core Ops, SparseCore 0:
  8.9 84.7 all-gather.5
  95.6 120.8 all-gather.7
  218.3 122.3 all-gather.9
  342.4 122.3 all-gather.11
  484.1 89.5 reduce-scatter.1
where the time goes:
time: 713 us; the launch traced here: 712 us
  waiting for transfers between devices  502 us (70%)
  local copies, waits for them, and re-layouts  82.9 us (12%)
  matrix products  65.3 us (9%)
  blocking collectives  39.5 us (6%)
  between operations  13.3 us (2%)
  other arithmetic  9.15 us (1%)
    all_gather x1, waiting for transfers between devices, local(): gate = add_one(lax.all_gather(gate_weight, 'batch', axis=0, tiled=True))  118 us
    all_gather x1, waiting for transfers between devices, local(): up = add_one(lax.all_gather(up_weight, 'batch', axis=0, tiled=True))  105 us
    all_gather x1, waiting for transfers between devices, local(): lax.all_gather(down_weight, 'batch', axis=1, tiled=True)  103 us
    reduce_scatter x1, waiting for transfers between devices, local(): lax.psum_scatter(terms.astype(jnp.bfloat16), 'corpus', scatter_dimension=...  89.4 us
    all_gather x1, waiting for transfers between devices, local(): whole = lax.all_gather(states, 'corpus', axis=1, tiled=True)  84.4 us
    gather x3, local copies, waits for them, and re-layouts, local(): scores = jnp.take_along_axis(table, my_index, axis=1)  82 us
    dot_general x2, matrix products, add_rows(): return jnp.dot(left, piece, preferred_element_type=jnp.float32)  40.3 us
    all_gather x1, blocking collectives, local(): gathered = lax.all_gather(codes, ('batch', 'corpus'), axis=0, tiled=True)  39.5 us
  transfers between devices with their start and end apart: 5, of which 5 were waited for; matrix products, arithmetic and copies ran while one was open for 6% of the time, Pallas kernels for 0%

commit v1 on v0

--- a/solution.py
+++ b/solution.py
@@ -31,7 +31,14 @@
     corpus_count = lax.axis_size("corpus")
     devices = lax.axis_size("batch") * corpus_count
     flat_index = lax.axis_index("batch") * corpus_count + lax.axis_index("corpus")
-    whole = lax.all_gather(states, "corpus", axis=1, tiled=True)
+    ring = [states]
+    for hop in range(7):
+        ring.append(lax.ppermute(ring[-1], "corpus", [(dev, (dev + 1) % 8) for dev in range(8)]))
+    whole = jnp.roll(
+        jnp.concatenate(ring[::-1], axis=1),
+        (lax.axis_index("corpus") + 1) * ring[0].shape[1],
+        axis=1,
+    )
     normed = rms(whole.astype(jnp.float32), norm_gain).astype(jnp.bfloat16)
 
     def add_one(piece):

time: 713 us -> 632 us (0.89)
  waiting for transfers between devices: 502 us -> 398 us
  local copies, waits for them, and re-layouts: 82.9 us -> 107 us
    all_gather x1, waiting for transfers between devices: 118 us -> 0.02 us  [local(): gate = add_one(lax.all_gather(gate_weight, 'batch', axis=0, tiled=True))]
    ppermute x0 -> x7, waiting for transfers between devices: none -> 113 us  [local(): lax.ppermute(ring[-1], 'corpus', [(dev, (dev + 1) % 8) for dev in range(8)])]
    all_gather x1 -> x0, waiting for transfers between devices: 84.4 us -> none  [local(): whole = lax.all_gather(states, 'corpus', axis=1, tiled=True)]
    unnamed x10 -> x49, local copies, waits for them, and re-layouts: 0.16 us -> 24.5 us
    all_gather x1, waiting for transfers between devices: 105 us -> 89.4 us  [local(): up = add_one(lax.all_gather(up_weight, 'batch', axis=0, tiled=True))]
  transfers between devices with their start and end apart: 5 -> 11, of which waited for: 5 -> 10; matrix products, arithmetic and copies ran while one was open for 6% -> 9% of each run, Pallas kernels for 0% -> 0%
where the time goes in v1:
time: 632 us; the launch traced here: 631 us
  waiting for transfers between devices  398 us (63%)
  local copies, waits for them, and re-layouts  107 us (17%)
  matrix products  65.9 us (10%)
  blocking collectives  39.5 us (6%)
  between operations  13.5 us (2%)
  other arithmetic  6.46 us (1%)
    ppermute x7, waiting for transfers between devices, local(): lax.ppermute(ring[-1], 'corpus', [(dev, (dev + 1) % 8) for dev in range(8)])  113 us
    all_gather x1, waiting for transfers between devices, local(): lax.all_gather(down_weight, 'batch', axis=1, tiled=True)  104 us
    all_gather x1, waiting for transfers between devices, local(): up = add_one(lax.all_gather(up_weight, 'batch', axis=0, tiled=True))  89.4 us
    reduce_scatter x1, waiting for transfers between devices, local(): lax.psum_scatter(terms.astype(jnp.bfloat16), 'corpus', scatter_dimension=...  89.4 us
    gather x3, local copies, waits for them, and re-layouts, local(): scores = jnp.take_along_axis(table, my_index, axis=1)  82 us
    dot_general x2, matrix products, add_rows(): return jnp.dot(left, piece, preferred_element_type=jnp.float32)  40.8 us
    all_gather x1, blocking collectives, local(): gathered = lax.all_gather(codes, ('batch', 'corpus'), axis=0, tiled=True)  39.5 us
    unnamed x49, local copies, waits for them, and re-layouts  24.5 us
  transfers between devices with their start and end apart: 11, of which 10 were waited for; matrix products, arithmetic and copies ran while one was open for 9% of the time, Pallas kernels for 0%

profile of v1, /device:TPU:0, one launch (start us, length us, event | category | flops | bytes accessed | tf_op | source)
XLA Modules:
  0.0 631.2 jit_solution(8917958217705613876)
XLA Ops:
  6.5 0.7 all-gather.5.cloned.1.call-update
  7.3 0.7 all-gather.7.cloned.1.call-update
  8.1 0.7 all-gather.9.cloned.1.call-update
  8.8 0.5 collective-permute-start
  9.3 16.7 %collective-permute-done = bf16[1024,512]{1,0:T(8,128)(2,1)S(1)} collective-permute-done((bf16[1024,512]{1,0:T(8,128)(2,1)}, bf16[1024,512]{1,0:T(8,128)(2,1)S(1)}, u32[]{:S(2)}, u32[]{:S(2)}) %collective-permute-start) | collective-permute-done | bytes 1048608 | tf_op jit(solution)/shard_map/ppermute | solution.py:36
  26.1 1.0 copy-done.3
  27.0 16.0 %collective-permute-done.1 = bf16[1024,512]{1,0:T(8,128)(2,1)S(1)} collective-permute-done((bf16[1024,512]{1,0:T(8,128)(2,1)S(1)}, bf16[1024,512]{1,0:T(8,128)(2,1)S(1)}, u32[]{:S(2)}, u32[]{:S(2)}) %collective-permute-start.1) | collective-permute-done | bytes 1048608 | tf_op jit(solution)/shard_map/ppermute | solution.py:36
  43.0 1.0 copy-done.5
  44.0 16.0 %collective-permute-done.2 = bf16[1024,512]{1,0:T(8,128)(2,1)S(1)} collective-permute-done((bf16[1024,512]{1,0:T(8,128)(2,1)S(1)}, bf16[1024,512]{1,0:T(8,128)(2,1)S(1)}, u32[]{:S(2)}, u32[]{:S(2)}) %collective-permute-start.2) | collective-permute-done | bytes 1048608 | tf_op jit(solution)/shard_map/ppermute | solution.py:36
  60.1 1.0 copy-done.7
  61.0 16.0 %collective-permute-done.3 = bf16[1024,512]{1,0:T(8,128)(2,1)S(1)} collective-permute-done((bf16[1024,512]{1,0:T(8,128)(2,1)S(1)}, bf16[1024,512]{1,0:T(8,128)(2,1)S(1)}, u32[]{:S(2)}, u32[]{:S(2)}) %collective-permute-start.3) | collective-permute-done | bytes 1048608 | tf_op jit(solution)/shard_map/ppermute | solution.py:36
  77.0 1.0 copy-done.9
  78.0 16.0 %collective-permute-done.4 = bf16[1024,512]{1,0:T(8,128)(2,1)S(1)} collective-permute-done((bf16[1024,512]{1,0:T(8,128)(2,1)S(1)}, bf16[1024,512]{1,0:T(8,128)(2,1)S(1)}, u32[]{:S(2)}, u32[]{:S(2)}) %collective-permute-start.4) | collective-permute-done | bytes 1048608 | tf_op jit(solution)/shard_map/ppermute | solution.py:36
  94.1 1.0 copy-done.11
  95.0 16.1 %collective-permute-done.5 = bf16[1024,512]{1,0:T(8,128)(2,1)} collective-permute-done((bf16[1024,512]{1,0:T(8,128)(2,1)S(1)}, bf16[1024,512]{1,0:T(8,128)(2,1)}, u32[]{:S(2)}, u32[]{:S(2)}) %collective-permute-start.5) | collective-permute-done | bytes 1048608 | tf_op jit(solution)/shard_map/ppermute | solution.py:36
  111.2 16.3 %collective-permute-done.6 = bf16[1024,512]{1,0:T(8,128)(2,1)} collective-permute-done((bf16[1024,512]{1,0:T(8,128)(2,1)}, bf16[1024,512]{1,0:T(8,128)(2,1)}, u32[]{:S(2)}, u32[]{:S(2)}) %collective-permute-start.6) | collective-permute-done | bytes 1048608 | tf_op jit(solution)/shard_map/ppermute | solution.py:36
  127.5 1.3 constant_dynamic-update-slice_fusion.15
  128.9 1.4 constant_dynamic-update-slice_fusion.14
  130.3 1.3 constant_dynamic-update-slice_fusion.13
  131.7 1.3 constant_dynamic-update-slice_fusion.12
  133.0 1.3 constant_dynamic-update-slice_fusion.11
  134.4 1.3 constant_dynamic-update-slice_fusion.10
  135.7 0.1 constant_dynamic-update-slice_fusion.9
  135.9 0.1 constant_dynamic-update-slice_fusion.8
  136.0 1.4 constant_dynamic-update-slice_fusion.7
  137.4 1.3 constant_dynamic-update-slice_fusion.6
  138.7 0.1 constant_dynamic-update-slice_fusion.5
  138.9 0.1 constant_dynamic-update-slice_fusion.4
  139.0 0.1 constant_dynamic-update-slice_fusion.3
  139.2 0.1 constant_dynamic-update-slice_fusion.2
  139.3 0.1 constant_dynamic-update-slice_fusion.1
  139.4 0.1 constant_dynamic-update-slice_fusion
  139.6 7.7 %copy-done.1 = bf16[1024,8192]{1,0:T(8,128)(2,1)} copy-done((bf16[1024,8192]{1,0:T(8,128)(2,1)}, bf16[1024,8192]{1,0:T(8,128)(2,1)S(1)}, u32[]{:S(2)}) %copy-start.1) | copy-done | bytes 16777240
  147.3 1.7 fusion
  149.1 20.1 %fusion.4 = f32[1024,1536]{1,0:T(8,128)} fusion(bf16[4096,1536]{1,0:T(8,128)(2,1)} %all-gather.5.cloned.1.call-done, f32[4096]{0:T(1024)S(1)} %copy-done.15, f32[1024]{0:T(1024)S(1)} %add_rsqrt_fusion, bf16[1024,8192]{1,0:T(8,128)(2,1)} %copy-done.1, s32[]{:T(128)S(6)} %select_n.37), kind=kOutput, calls=%fused_computation.12 | convolution fusion | flops 12901679104 | bytes 27283460 | tf_op jit(solution)/shard_map/dot_general | solution.py:16
  169.1 89.4 %all-gather.7.cloned.1.call-done = bf16[4096,1536]{1,0:T(8,128)(2,1)} async-done(((bf16[1024,1536]{1,0:T(8,128)(2,1)}), bf16[4096,1536]{1,0:T(8,128)(2,1)}) %all-gather.7.cloned.1.call-update) | async-done | bytes 12582928 | tf_op jit(solution)/shard_map/all_gather | solution.py:48
  258.6 20.7 %multiply_convert_fusion = bf16[1024,1536]{1,0:T(8,128)(2,1)} fusion(f32[1024,1536]{1,0:T(8,128)} %fusion.4, bf16[4096,1536]{1,0:T(8,128)(2,1)} %all-gather.7.cloned.1.call-done, f32[4096]{0:T(1024)S(1)} %copy-done.15, f32[1024]{0:T(1024)S(1)} %add_rsqrt_fusion, bf16[1024,8192]{1,0:T(8,128)(2,1)} %copy-done.1, s32[]{:T(128)S(6)} %select_n.37), kind=kOutput, calls=%fused_computation.7 | convolution fusion | flops 12911116288 | bytes 30429188 | tf_op jit(solution)/shard_map/dot_general | solution.py:16
  279.2 103.6 %all-gather.9.cloned.1.call-done = bf16[1536,4096]{1,0:T(8,128)(2,1)} async-done(((bf16[1536,1024]{1,0:T(8,128)(2,1)}), bf16[1536,4096]{1,0:T(8,128)(2,1)}) %all-gather.9.cloned.1.call-update) | async-done | bytes 12582928 | tf_op jit(solution)/shard_map/all_gather | solution.py:52
  382.8 19.1 %convolution_convert_fusion = bf16[1024,4096]{1,0:T(8,128)(2,1)} fusion(bf16[1024,1536]{1,0:T(8,128)(2,1)} %multiply_convert_fusion, bf16[1536,4096]{1,0:T(8,128)(2,1)} %all-gather.9.cloned.1.call-done), kind=kOutput, calls=%fused_computation.6 | convolution fusion | flops 12889096192 | bytes 24117248 | tf_op jit(solution)/shard_map/dot_general | solution.py:50
  402.3 89.4 %reduce-scatter.2.cloned.1.call-done = bf16[128,4096]{1,0:T(8,128)(2,1)} async-done(((bf16[1024,4096]{1,0:T(8,128)(2,1)}), bf16[128,4096]{1,0:T(8,128)(2,1)}) %reduce-scatter.2.cloned.1.call-update) | async-done | bytes 1048592 | tf_op jit(solution)/shard_map/reduce_scatter | solution.py:55
  491.6 2.3 multiply_reduce_fusion
  494.0 2.4 bitcast_reduce_fusion
  496.4 4.6 fusion.9
  501.0 39.5 %all-gather = bf16[32,2,1024]{2,1,0:T(2,128)(2,1)S(1)} all-gather(bf16[1,2,1024]{2,1,0:T(2,128)(2,1)S(1)} %fusion.9), channel_id=1, replica_groups=mesh['batch'=4,'corpus'=8] {'batch','corpus'}, dimensions={0}, use_global_device_ids=true | all-gather | bytes 135168 | tf_op jit(solution)/shard_map/all_gather | solution.py:71
  540.5 1.4 fusion.7
  541.9 81.8 %gather_fusion = f32[12800]{0:T(1024)S(1)} fusion(f32[128,64]{0,1:T(8,128)S(1)} %fusion.7, s32[12800]{0:T(1024)S(1)} %reshape.33), kind=kCustom, calls=%fused_computation | custom fusion | bytes 204800 | tf_op jit(solution)/shard_map/jit(take_along_axis)/gather | solution.py:82
  623.7 0.1 reshape.36
  623.9 0.7 copy.14
  (46 shorter events, 0.6 us)
Async XLA Ops:
  6.5 395.4 %copy-start = (s32[4096,100]{0,1:T(8,128)S(1)}, s32[4096,100]{0,1:T(8,128)}, u32[]{:S(2)}) copy-start(s32[4096,100]{0,1:T(8,128)} %param.19) | copy-start | bytes 4915204
  6.5 129.3 %copy-start.2 = (bf16[1024,512]{1,0:T(8,128)(2,1)S(1)}, bf16[1024,512]{1,0:T(8,128)(2,1)}, u32[]{:S(2)}) copy-start(bf16[1024,512]{1,0:T(8,128)(2,1)} %param.10) | copy-start | bytes 3145732
  6.5 142.5 %all-gather.5.cloned.1.call-start = ((), (), s32[]{:S(2)}) async-start(), calls=%async_computation.1 | async-start | bytes 15728640 | tf_op jit(solution)/shard_map/all_gather | solution.py:47
  7.3 251.3 %all-gather.7.cloned.1.call-start = ((), (), s32[]{:S(2)}) async-start(), calls=%async_computation.2 | async-start | bytes 15728640 | tf_op jit(solution)/shard_map/all_gather | solution.py:48
  8.0 374.8 %all-gather.9.cloned.1.call-start = ((), (), s32[]{:S(2)}) async-start(), calls=%async_computation.3 | async-start | bytes 15728640 | tf_op jit(solution)/shard_map/all_gather | solution.py:52
  8.7 482.9 %reduce-scatter.2.cloned.1.call-start = ((), (), s32[]{:S(2)}) async-start(), calls=%async_computation.4 | async-start | bytes 9437184 | tf_op jit(solution)/shard_map/reduce_scatter | solution.py:55
  8.8 17.3 %collective-permute-start = (bf16[1024,512]{1,0:T(8,128)(2,1)}, bf16[1024,512]{1,0:T(8,128)(2,1)S(1)}, u32[]{:S(2)}, u32[]{:S(2)}) collective-permute-start(bf16[1024,512]{1,0:T(8,128)(2,1)} %param.10), channel_id=1, source_target_pairs={{0,1},{1,2},{2,3},{3,4},{4,5},{5,6},{6,7},{7,0},{8,9},{9,10},{10,1... | collective-permute-start | bytes 3145736 | tf_op jit(solution)/shard_map/ppermute | solution.py:36
  26.1 1.0 copy-start.3
  27.0 16.0 %collective-permute-start.1 = (bf16[1024,512]{1,0:T(8,128)(2,1)S(1)}, bf16[1024,512]{1,0:T(8,128)(2,1)S(1)}, u32[]{:S(2)}, u32[]{:S(2)}) collective-permute-start(bf16[1024,512]{1,0:T(8,128)(2,1)S(1)} %collective-permute-done), channel_id=1, source_target_pairs={{0,1},{1,2},{2,3},{3,4},{4,5},{5,6},{6,7},{7,0},{8,9},{9,10},{10,1... | collective-permute-start | bytes 3145736 | tf_op jit(solution)/shard_map/ppermute | solution.py:36
  43.0 1.0 copy-start.5
  44.0 16.0 %collective-permute-start.2 = (bf16[1024,512]{1,0:T(8,128)(2,1)S(1)}, bf16[1024,512]{1,0:T(8,128)(2,1)S(1)}, u32[]{:S(2)}, u32[]{:S(2)}) collective-permute-start(bf16[1024,512]{1,0:T(8,128)(2,1)S(1)} %collective-permute-done.1), channel_id=1, source_target_pairs={{0,1},{1,2},{2,3},{3,4},{4,5},{5,6},{6,7},{7,0},{8,9},{9,10},{10,1... | collective-permute-start | bytes 3145736 | tf_op jit(solution)/shard_map/ppermute | solution.py:36
  60.1 1.0 copy-start.7
  61.0 16.0 %collective-permute-start.3 = (bf16[1024,512]{1,0:T(8,128)(2,1)S(1)}, bf16[1024,512]{1,0:T(8,128)(2,1)S(1)}, u32[]{:S(2)}, u32[]{:S(2)}) collective-permute-start(bf16[1024,512]{1,0:T(8,128)(2,1)S(1)} %collective-permute-done.2), channel_id=1, source_target_pairs={{0,1},{1,2},{2,3},{3,4},{4,5},{5,6},{6,7},{7,0},{8,9},{9,10},{10,1... | collective-permute-start | bytes 3145736 | tf_op jit(solution)/shard_map/ppermute | solution.py:36
  77.0 1.0 copy-start.9
  78.0 16.0 %collective-permute-start.4 = (bf16[1024,512]{1,0:T(8,128)(2,1)S(1)}, bf16[1024,512]{1,0:T(8,128)(2,1)S(1)}, u32[]{:S(2)}, u32[]{:S(2)}) collective-permute-start(bf16[1024,512]{1,0:T(8,128)(2,1)S(1)} %collective-permute-done.3), channel_id=1, source_target_pairs={{0,1},{1,2},{2,3},{3,4},{4,5},{5,6},{6,7},{7,0},{8,9},{9,10},{10,1... | collective-permute-start | bytes 3145736 | tf_op jit(solution)/shard_map/ppermute | solution.py:36
  94.1 1.0 copy-start.11
  95.0 16.1 %collective-permute-start.5 = (bf16[1024,512]{1,0:T(8,128)(2,1)S(1)}, bf16[1024,512]{1,0:T(8,128)(2,1)}, u32[]{:S(2)}, u32[]{:S(2)}) collective-permute-start(bf16[1024,512]{1,0:T(8,128)(2,1)S(1)} %collective-permute-done.4), channel_id=1, source_target_pairs={{0,1},{1,2},{2,3},{3,4},{4,5},{5,6},{6,7},{7,0},{8,9},{9,10},{10,1... | collective-permute-start | bytes 3145736 | tf_op jit(solution)/shard_map/ppermute | solution.py:36
  111.2 16.3 %collective-permute-start.6 = (bf16[1024,512]{1,0:T(8,128)(2,1)}, bf16[1024,512]{1,0:T(8,128)(2,1)}, u32[]{:S(2)}, u32[]{:S(2)}) collective-permute-start(bf16[1024,512]{1,0:T(8,128)(2,1)} %collective-permute-done.5), channel_id=1, source_target_pairs={{0,1},{1,2},{2,3},{3,4},{4,5},{5,6},{6,7},{7,0},{8,9},{9,10},{10,1... | collective-permute-start | bytes 3145736 | tf_op jit(solution)/shard_map/ppermute | solution.py:36
  111.2 24.6 %copy-start.4 = (bf16[1024,512]{1,0:T(8,128)(2,1)S(1)}, bf16[1024,512]{1,0:T(8,128)(2,1)}, u32[]{:S(2)}) copy-start(bf16[1024,512]{1,0:T(8,128)(2,1)} %copy-done.3) | copy-start | bytes 3145732
  111.2 27.6 %copy-start.12 = (bf16[1024,512]{1,0:T(8,128)(2,1)S(1)}, bf16[1024,512]{1,0:T(8,128)(2,1)}, u32[]{:S(2)}) copy-start(bf16[1024,512]{1,0:T(8,128)(2,1)} %copy-done.11) | copy-start | bytes 3145732
  111.2 27.7 %copy-start.10 = (bf16[1024,512]{1,0:T(8,128)(2,1)S(1)}, bf16[1024,512]{1,0:T(8,128)(2,1)}, u32[]{:S(2)}) copy-start(bf16[1024,512]{1,0:T(8,128)(2,1)} %copy-done.9) | copy-start | bytes 3145732
  111.2 27.8 %copy-start.8 = (bf16[1024,512]{1,0:T(8,128)(2,1)S(1)}, bf16[1024,512]{1,0:T(8,128)(2,1)}, u32[]{:S(2)}) copy-start(bf16[1024,512]{1,0:T(8,128)(2,1)} %copy-done.7) | copy-start | bytes 3145732
  128.9 10.3 %copy-start.6 = (bf16[1024,512]{1,0:T(8,128)(2,1)S(1)}, bf16[1024,512]{1,0:T(8,128)(2,1)}, u32[]{:S(2)}) copy-start(bf16[1024,512]{1,0:T(8,128)(2,1)} %copy-done.5) | copy-start | bytes 3145732
  136.0 13.0 %copy-start.15 = (f32[4096]{0:T(1024)S(1)}, f32[4096]{0:T(1024)}, u32[]{:S(2)}) copy-start(f32[4096]{0:T(1024)} %param.11) | copy-start | bytes 49156
  139.6 7.8 %copy-start.1 = (bf16[1024,8192]{1,0:T(8,128)(2,1)}, bf16[1024,8192]{1,0:T(8,128)(2,1)S(1)}, u32[]{:S(2)}) copy-start(bf16[1024,8192]{1,0:T(8,128)(2,1)S(1)} %constant_dynamic-update-slice_fusion) | copy-start | bytes 50331652
  279.2 214.7 %copy-start.13 = (f32[4096]{0:T(1024)S(1)}, f32[4096]{0:T(1024)}, u32[]{:S(2)}) copy-start(f32[4096]{0:T(1024)} %param.15) | copy-start | bytes 49156
  401.9 138.6 %copy-start.14 = (s32[64]{0:T(128)S(1)}, s32[64]{0:T(128)}, u32[]{:S(2)}) copy-start(s32[64]{0:T(128)} %param.18) | copy-start | bytes 772
Sparse Core Ops, SparseCore 0:
  9.2 125.0 all-gather.4
  136.2 122.3 all-gather.6
  260.4 122.3 all-gather.8
  402.1 89.5 reduce-scatter.1
